TPU v7x, 512 devices: a whole 4x8x8 slice. The times are simulated.
512 devices in a mesh: node: 8 (over y_hi, core), slab: 64 (over y_lo, x, z).
Axes of the slice: x: 4, y: 8 (y_hi: 4, y_lo: 2; y = y_hi * 2 + y_lo), z: 8, core: 2. Of those that a mesh axis runs over, the one named last changes fastest.
Arguments:
- adjoint_source: float32 [8, 6, 256, 64, 256], P('node', None, 'slab'), may hold values from -6 to 6
- stencil_coef: float32 [8, 4, 256, 64, 256], P('node', None, 'slab'), may hold values from 0.05 to 0.5
- flux_block: float32 [8, 6, 6], P('node'), may hold values from -1.25 to 1.25
- shape_metric: float32 [8, 6, 256, 64, 256], P('node', None, 'slab'), may hold values from -0.3125 to 0.3125
- wall_force: float32 [8, 256, 256], P('node', 'slab'), may hold values from -8 to 8
Outputs:
- wall_gradient: float32 [256, 256], P('slab', 'node')
All inputs are finite; a program needn't handle non-finite values.
Results may differ from a plain program's by a relative error of at most 0.00014.
Values sent between devices are 32-bit elements; how exact they have to be, the bound alone decides.
A program may use at most 64 MiB of HBM per device.

v0:
```python
import math

import jax
import jax.numpy as jnp
from jax import lax
from jax.sharding import PartitionSpec as P

ITERS = 3


def with_halo(block, sides, width):
    for axis, dim in sides:
        count = lax.axis_size(axis)
        forward = [(i, i + 1) for i in range(count - 1)]
        backward = [(target, source) for source, target in forward]
        low = lax.ppermute(
            lax.slice_in_dim(block, block.shape[dim] - width, None, axis=dim), axis, forward
        )
        high = lax.ppermute(lax.slice_in_dim(block, 0, width, axis=dim), axis, backward)
        block = jnp.concatenate([low, block, high], axis=dim)
    return block


def sweep(extended, source, coef, diag, block):
    padded = jnp.pad(extended, ((0, 0), (0, 0), (1, 1), (1, 1)))
    middle = padded[:, 1:-1, 1:-1, 1:-1]
    coupled = coef[1] * (padded[:, 2:, 1:-1, 1:-1] + padded[:, :-2, 1:-1, 1:-1])
    coupled = coupled + coef[2] * (padded[:, 1:-1, 2:, 1:-1] + padded[:, 1:-1, :-2, 1:-1])
    coupled = coupled + coef[3] * (padded[:, 1:-1, 1:-1, 2:] + padded[:, 1:-1, 1:-1, :-2])
    mixed = jnp.einsum("vw,vxyz->wxyz", block, coupled, precision=lax.Precision.HIGHEST)
    return middle + (source - (diag * middle - mixed)) / diag


def per_device(adjoint_source, stencil_coef, flux_block, shape_metric, wall_force):
    source = adjoint_source[0]
    coef = stencil_coef[0]
    block = flux_block[0]
    sweeps = ITERS - 1
    diag = 0.5 + coef[0] + 2.4 * (coef[1] + coef[2] + coef[3])
    psi = source / diag
    for step in range(sweeps):
        extended = with_halo(psi, (("slab", 1),), 1)
        psi = sweep(extended, source, coef, diag, block)
    sens = jnp.sum(psi * shape_metric[0], axis=(0, 2))
    nodes = lax.axis_size("node")
    cells = wall_force.shape[1] * lax.axis_size("slab") * wall_force.shape[2]
    local_sum = jnp.sum(wall_force[0])
    node_sum = lax.psum(local_sum, "slab")
    objective = lax.all_gather(jnp.reshape(node_sum / cells, (1,)), "node", axis=0, tiled=True)
    order = jnp.arange(nodes, dtype=jnp.float32)
    weight = jnp.sin(math.pi * (order + 0.5) / nodes)
    weight = weight / jnp.sum(weight)
    mean_value = jnp.sum(weight * objective)
    variance = jnp.sum(weight * (objective - mean_value) ** 2)
    spread = jnp.sqrt(variance + 0.25)
    factor = weight * (1.0 + 2.0 * (objective - mean_value) / spread)
    mine = jnp.sum(jnp.where(jnp.arange(nodes) == lax.axis_index("node"), factor, 0.0))
    term = mine * sens
    total = lax.psum(term, "node")
    width = term.shape[1] // nodes
    return lax.dynamic_slice_in_dim(total, lax.axis_index("node") * width, width, 1)


def solution(mesh):
    return jax.shard_map(
        per_device,
        mesh=mesh,
        in_specs=(
            P("node", None, "slab", None, None),
            P("node", None, "slab", None, None),
            P("node", None, None),
            P("node", None, "slab", None, None),
            P("node", "slab", None),
        ),
        out_specs=P("slab", "node"),
        check_vma=False,
    )
```

profile of v0, /device:TPU:8, one launch (start us, length us, event | category | flops | bytes accessed | tf_op | source)
XLA Modules:
  0.0 262.3 jit_solution(4892447535925835626)
XLA Ops:
  0.0 1.3 bitcast_add_fusion
  1.3 0.0 copy-start
  1.3 2.5 bitcast_divide_fusion
  3.7 0.1 fusion.57
  3.8 13.0 %collective-permute-start = (f32[6,1,64,256]{3,0,2,1:T(8,128)S(1)}, f32[6,1,64,256]{3,0,2,1:T(8,128)S(1)}, u32[]{:S(2)}, u32[]{:S(2)}) collective-permute-start(f32[6,1,64,256]{3,0,2,1:T(8,128)S(1)} %get-tuple-element.8), channel_id=1, source_target_pairs={{1,0},{2,1},{3,2},{4,3},{5,4},{6,5},{7,6},{8,7},{9,8},{10,9},{11,1... | collective-permute-start | bytes 1179656 | tf_op jit(solution)/shard_map/ppermute | solution.py:19
  16.9 1.9 collective-permute-start.1
  18.8 0.0 copy-done
  18.8 0.1 slice_bitcast_fusion.2
  18.9 0.0 copy-start.3
  18.9 0.0 copy-start.5
  18.9 0.0 copy-start.7
  18.9 0.0 copy-start.1
  18.9 0.0 copy-start.11
  18.9 9.1 %collective-permute-done = f32[6,1,64,256]{3,0,2,1:T(8,128)S(1)} collective-permute-done((f32[6,1,64,256]{3,0,2,1:T(8,128)S(1)}, f32[6,1,64,256]{3,0,2,1:T(8,128)S(1)}, u32[]{:S(2)}, u32[]{:S(2)}) %collective-permute-start) | collective-permute-done | bytes 393248 | tf_op jit(solution)/shard_map/ppermute | solution.py:19
  28.0 8.3 %collective-permute-done.1 = f32[6,1,64,256]{3,0,2,1:T(8,128)S(1)} collective-permute-done((f32[6,1,64,256]{3,0,2,1:T(8,128)S(1)}, f32[6,1,64,256]{3,0,2,1:T(8,128)S(1)}, u32[]{:S(2)}, u32[]{:S(2)}) %collective-permute-start.1) | collective-permute-done | bytes 393248 | tf_op jit(solution)/shard_map/ppermute | solution.py:16
  36.4 2.2 select_maximum_fusion.2
  38.5 0.0 copy-done.3
  38.5 0.0 copy-done.5
  38.6 0.0 copy-done.7
  38.6 0.0 copy-done.1
  38.6 0.0 copy-done.11
  38.6 6.5 %fusion.37 = f32[6,4,64,256]{3,0,2,1:T(8,128)S(1)} fusion(f32[6,4,64,256]{3,0,2,1:T(8,128)S(1)} %bitcast_divide_fusion, f32[1,6,4,64,256]{4,3,2,1,0:T(8,128)S(1)} %copy-done.1, f32[6,6,66,258]{3,0,2,1:T(8,128)S(1)} %select_maximum_fusion.2, f32[6,1,64,256]{3,0,2,1:T(8,128)S(1)} %collective-permute-done.1, f32[6,1,64,256]{3,0,2,1:T(8,128)S(1)} %collective-permute-done, ...), kind=kOutput, calls=%fused_computation.50 | convolution fusion | flops 34209792 | bytes 17828864 | tf_op jit(solution)/shard_map/vw,vxyz->wxyz/dot_general | solution.py:30
  45.1 0.0 copy-start.9
  45.1 0.1 fusion.56
  45.1 1.9 collective-permute-start.2
  47.1 3.9 %collective-permute-start.3 = (f32[6,1,64,256]{3,0,2,1:T(8,128)S(1)}, f32[6,1,64,256]{3,0,2,1:T(8,128)}, u32[]{:S(2)}, u32[]{:S(2)}) collective-permute-start(f32[6,1,64,256]{3,0,2,1:T(8,128)S(1)} %get-tuple-element.5), channel_id=1, source_target_pairs={{0,1},{1,2},{2,3},{3,4},{4,5},{5,6},{6,7},{7,8},{8,9},{9,10},{10,1... | collective-permute-start | bytes 1179656 | tf_op jit(solution)/shard_map/ppermute | solution.py:16
  51.0 0.0 copy-done.9
  51.0 0.6 reduce_sum.55
  51.6 157.7 %psum.14 = f32[]{:T(128)} all-reduce(f32[]{:T(128)} %reduce_sum.55), channel_id=1, replica_groups=mesh['node'=8,'slab'=64] {'slab'}, use_global_device_ids=true, to_apply=%region_2.3 | all-reduce | flops 1 | bytes 8 | tf_op jit(solution)/shard_map/psum | solution.py:48
  209.3 1.3 dynamic-slice
  211.2 0.7 dynamic-update-slice
  211.9 14.2 %all-reduce.2 = f32[8]{0:T(128)S(1)} all-reduce(f32[8]{0:T(128)S(1)} %dynamic-update-slice), channel_id=1, replica_groups=mesh['node'=8,'slab'=64] {'node'}, use_global_device_ids=true, to_apply=%add.2 | all-reduce | flops 8 | bytes 64
  226.1 0.6 fusion.53
  226.8 1.4 multiply_reduce_fusion.1
  228.2 2.0 multiply_reduce_fusion
  230.8 2.0 fusion.52
  232.8 0.0 copy-start.2
  232.8 0.0 copy-start.4
  232.8 0.0 copy-start.6
  232.8 0.0 copy-start.8
  232.8 0.0 copy-start.10
  232.8 0.0 collective-permute-done.2
  232.8 0.0 collective-permute-done.3
  232.8 3.4 %select_maximum_fusion = f32[6,6,66,258]{3,0,2,1:T(8,128)S(1)} fusion(f32[6,1,64,256]{3,0,2,1:T(8,128)} %collective-permute-done.2, f32[6,4,64,256]{3,0,2,1:T(8,128)S(1)} %fusion.37, f32[6,1,64,256]{3,0,2,1:T(8,128)} %collective-permute-done.3), kind=kLoop, calls=%fused_computation.4 | loop fusion | flops 9195120 | bytes 4811328 | tf_op jit(solution)/shard_map/concatenate | solution.py:20
  236.2 0.0 copy-done.2
  236.2 0.0 copy-done.4
  236.2 0.0 copy-done.6
  236.2 0.0 copy-done.8
  236.2 0.0 copy-done.10
  236.2 9.1 %fusion.31 = f32[4,256]{1,0:T(4,128)S(1)} fusion(f32[6,4,64,256]{3,0,2,1:T(8,128)S(1)} %fusion.37, f32[1,6,4,64,256]{4,3,2,1,0:T(8,128)S(1)} %copy-done.2, f32[1,6,4,64,256]{4,3,2,1,0:T(8,128)S(1)} %copy-done.10, f32[6,6,66,258]{3,0,2,1:T(8,128)S(1)} %select_maximum_fusion, f32[6,1,64,256]{3,0,2,1:T(8,128)} %collective-permute-done.3, ...), kind=kOutput, calls=%fused_computation.42 | convolution fusion | flops 34995200 | bytes 17570816 | tf_op jit(solution)/shard_map/vw,vxyz->wxyz/dot_general | solution.py:30
  245.3 0.6 broadcast_multiply_fusion
  245.9 15.8 %psum.15 = f32[4,256]{1,0:T(4,128)S(1)} all-reduce(f32[4,256]{1,0:T(4,128)S(1)} %broadcast_multiply_fusion), channel_id=1, replica_groups=mesh['node'=8,'slab'=64] {'node'}, use_global_device_ids=true, to_apply=%region_7.8 | all-reduce | flops 1024 | bytes 8192 | tf_op jit(solution)/shard_map/psum | solution.py:59
  261.7 0.7 constant_dynamic-slice_fusion
  (1 shorter events, 0.0 us)
Async XLA Ops:
  1.3 17.5 %copy-start = (f32[1,4,4,64,256]{4,3,2,1,0:T(8,128)S(1)}, f32[1,4,4,64,256]{4,3,2,1,0:T(8,128)}, u32[]{:S(2)}) copy-start(f32[1,4,4,64,256]{4,3,2,1,0:T(8,128)} %param.6) | copy-start | bytes 3145732
  3.8 24.2 %collective-permute-start = (f32[6,1,64,256]{3,0,2,1:T(8,128)S(1)}, f32[6,1,64,256]{3,0,2,1:T(8,128)S(1)}, u32[]{:S(2)}, u32[]{:S(2)}) collective-permute-start(f32[6,1,64,256]{3,0,2,1:T(8,128)S(1)} %get-tuple-element.8), channel_id=1, source_target_pairs={{1,0},{2,1},{3,2},{4,3},{5,4},{6,5},{7,6},{8,7},{9,8},{10,9},{11,1... | collective-permute-start | bytes 1179656 | tf_op jit(solution)/shard_map/ppermute | solution.py:19
  16.9 19.5 %collective-permute-start.1 = (f32[6,1,64,256]{3,0,2,1:T(8,128)S(1)}, f32[6,1,64,256]{3,0,2,1:T(8,128)S(1)}, u32[]{:S(2)}, u32[]{:S(2)}) collective-permute-start(f32[6,1,64,256]{3,0,2,1:T(8,128)S(1)} %get-tuple-element.7), channel_id=1, source_target_pairs={{0,1},{1,2},{2,3},{3,4},{4,5},{5,6},{6,7},{7,8},{8,9},{9,10},{10,1... | collective-permute-start | bytes 1179656 | tf_op jit(solution)/shard_map/ppermute | solution.py:16
  18.9 19.7 %copy-start.3 = (f32[4,64,256]{2,1,0:T(8,128)}, f32[4,64,256]{2,1,0:T(8,128)S(1)}, u32[]{:S(2)}) copy-start(f32[4,64,256]{2,1,0:T(8,128)S(1)} %get-tuple-element.9) | copy-start | bytes 786436
  18.9 19.7 %copy-start.5 = (f32[4,64,256]{2,1,0:T(8,128)}, f32[4,64,256]{2,1,0:T(8,128)S(1)}, u32[]{:S(2)}) copy-start(f32[4,64,256]{2,1,0:T(8,128)S(1)} %get-tuple-element.10) | copy-start | bytes 786436
  18.9 19.7 %copy-start.7 = (f32[4,64,256]{2,1,0:T(8,128)}, f32[4,64,256]{2,1,0:T(8,128)S(1)}, u32[]{:S(2)}) copy-start(f32[4,64,256]{2,1,0:T(8,128)S(1)} %get-tuple-element.11) | copy-start | bytes 786436
  18.9 19.7 %copy-start.1 = (f32[1,6,4,64,256]{4,3,2,1,0:T(8,128)S(1)}, f32[1,6,4,64,256]{4,3,2,1,0:T(8,128)}, u32[]{:S(2)}) copy-start(f32[1,6,4,64,256]{4,3,2,1,0:T(8,128)} %param.5) | copy-start | bytes 4718596
  18.9 19.7 %copy-start.11 = (f32[1,6,6]{2,0,1:T(1,128)S(1)}, f32[1,6,6]{2,0,1:T(1,128)}, u32[]{:S(2)}) copy-start(f32[1,6,6]{2,0,1:T(1,128)} %param.7) | copy-start | bytes 436
  45.1 6.0 %copy-start.9 = (f32[1,4,256]{2,1,0:T(4,128)S(1)}, f32[1,4,256]{2,1,0:T(4,128)}, u32[]{:S(2)}) copy-start(f32[1,4,256]{2,1,0:T(4,128)} %param.9) | copy-start | bytes 12292
  45.1 187.6 %collective-permute-start.2 = (f32[6,1,64,256]{3,0,2,1:T(8,128)S(1)}, f32[6,1,64,256]{3,0,2,1:T(8,128)}, u32[]{:S(2)}, u32[]{:S(2)}) collective-permute-start(f32[6,1,64,256]{3,0,2,1:T(8,128)S(1)} %get-tuple-element.6), channel_id=1, source_target_pairs={{1,0},{2,1},{3,2},{4,3},{5,4},{6,5},{7,6},{8,7},{9,8},{10,9},{11,1... | collective-permute-start | bytes 1179656 | tf_op jit(solution)/shard_map/ppermute | solution.py:19
  47.1 185.7 %collective-permute-start.3 = (f32[6,1,64,256]{3,0,2,1:T(8,128)S(1)}, f32[6,1,64,256]{3,0,2,1:T(8,128)}, u32[]{:S(2)}, u32[]{:S(2)}) collective-permute-start(f32[6,1,64,256]{3,0,2,1:T(8,128)S(1)} %get-tuple-element.5), channel_id=1, source_target_pairs={{0,1},{1,2},{2,3},{3,4},{4,5},{5,6},{6,7},{7,8},{8,9},{9,10},{10,1... | collective-permute-start | bytes 1179656 | tf_op jit(solution)/shard_map/ppermute | solution.py:16
  232.8 3.4 %copy-start.2 = (f32[1,6,4,64,256]{4,3,2,1,0:T(8,128)S(1)}, f32[1,6,4,64,256]{4,3,2,1,0:T(8,128)}, u32[]{:S(2)}) copy-start(f32[1,6,4,64,256]{4,3,2,1,0:T(8,128)} %param.5) | copy-start | bytes 4718596
  232.8 3.4 %copy-start.4 = (f32[4,64,256]{2,1,0:T(8,128)S(1)}, f32[4,64,256]{2,1,0:T(8,128)}, u32[]{:S(2)}) copy-start(f32[4,64,256]{2,1,0:T(8,128)} %copy-done.3) | copy-start | bytes 786436
  232.8 3.4 %copy-start.6 = (f32[4,64,256]{2,1,0:T(8,128)S(1)}, f32[4,64,256]{2,1,0:T(8,128)}, u32[]{:S(2)}) copy-start(f32[4,64,256]{2,1,0:T(8,128)} %copy-done.5) | copy-start | bytes 786436
  232.8 3.5 %copy-start.8 = (f32[4,64,256]{2,1,0:T(8,128)S(1)}, f32[4,64,256]{2,1,0:T(8,128)}, u32[]{:S(2)}) copy-start(f32[4,64,256]{2,1,0:T(8,128)} %copy-done.7) | copy-start | bytes 786436
  232.8 3.5 %copy-start.10 = (f32[1,6,4,64,256]{4,3,2,1,0:T(8,128)S(1)}, f32[1,6,4,64,256]{4,3,2,1,0:T(8,128)}, u32[]{:S(2)}) copy-start(f32[1,6,4,64,256]{4,3,2,1,0:T(8,128)} %param.8) | copy-start | bytes 4718596
where the time goes:
time: 263 us; the launch traced here: 262 us
  blocking collectives  188 us (71%)
  starting transfers between devices  20.8 us (8%)
  waiting for transfers between devices  17.4 us (7%)
  other arithmetic  16.5 us (6%)
  matrix products  15.5 us (6%)
  local copies, waits for them, and re-layouts  2.86 us (1%)
    psum x1, blocking collectives, per_device(): node_sum = lax.psum(local_sum, 'slab')  158 us
    psum x1, blocking collectives, per_device(): total = lax.psum(term, 'node')  15.8 us
    dot_general x2, matrix products, sweep(): jnp.einsum('vw,vxyz->wxyz', block, coupled, precision=lax.Precision.HIGHEST)  15.5 us
    ppermute x2, starting transfers between devices, with_halo(): lax.ppermute(lax.slice_in_dim(block, 0, width, axis=dim), axis, backward)  15 us
    unnamed x1, blocking collectives  14.2 us
    ppermute x2, waiting for transfers between devices, with_halo(): lax.ppermute(lax.slice_in_dim(block, 0, width, axis=dim), axis, backward)  9.11 us
    ppermute x2, waiting for transfers between devices, with_halo(): lax.ppermute(lax.slice_in_dim(block, block.shape[dim] - width, None, axis...  8.34 us
    ppermute x2, starting transfers between devices, with_halo(): lax.ppermute(lax.slice_in_dim(block, block.shape[dim] - width, None, axis...  5.84 us
  transfers between devices with their start and end apart: 4, of which 2 were waited for; matrix products, arithmetic and copies ran while one was open for 3% of the time, Pallas kernels for 0%

commit v1 on v0

v1 whole, which is shorter than its diff:
```python
import functools
import math

import jax
import jax.numpy as jnp
from jax import lax
from jax.experimental import pallas as pl
from jax.experimental.pallas import tpu as pltpu
from jax.sharding import PartitionSpec as P

MESH = pl.DeviceIdType.MESH
CHUNKS = 2
ROWS = 16
LANES = 128


def shifted_pairs(p):
    ny, nz = p.shape
    row = lax.broadcasted_iota(jnp.int32, p.shape, 0)
    lane = lax.broadcasted_iota(jnp.int32, p.shape, 1)
    above = jnp.where(row == 0, 0.0, pltpu.roll(p, 1, 0))
    below = jnp.where(row == ny - 1, 0.0, pltpu.roll(p, ny - 1, 0))
    before = jnp.where(lane == 0, 0.0, pltpu.roll(p, 1, 1))
    after = jnp.where(lane == nz - 1, 0.0, pltpu.roll(p, nz - 1, 1))
    return above + below, before + after


def fold_rows(block):
    return jnp.sum(jnp.reshape(block, (block.shape[0] // 8, 8, block.shape[1])), axis=0)


def kernel(
    nodes, slabs, inner, cells,
    source, coef, flux, shape, wall, out,
    psi0, cf, psi1, mix, tv, halo0, halo1, acc, wallv, obj, objn, own, sens, fin,
    load_sem, send0, recv0, send1, recv1, obj_send, obj_recv, fin_send, fin_recv,
):
    me, nd = lax.axis_index("slab"), lax.axis_index("node")
    outer = slabs // inner
    place, group = lax.rem(me, inner), lax.div(me, inner)
    right, left = lax.rem(me + 1, slabs), lax.rem(me + slabs - 1, slabs)
    nv, nx, ny, nz = psi0.shape
    part = ny // CHUNKS

    peers = [
        [{"slab": group * inner + lax.rem(place + d, inner)} for d in range(1, inner)],
        [{"slab": lax.rem(group + d, outer) * inner + place} for d in range(1, outer)],
        [{"node": lax.rem(nd + d, nodes)} for d in range(1, nodes)],
    ]

    barrier = pltpu.get_barrier_semaphore()
    everyone = [{"slab": left}, {"slab": right}] + peers[0] + peers[1] + peers[2]
    for peer in everyone:
        pl.semaphore_signal(barrier, inc=1, device_id=peer, device_id_type=MESH)

    loads = {}

    def load(name, src, dst, index):
        loads[name] = pltpu.make_async_copy(src, dst, load_sem.at[index])
        loads[name].start()

    load("wall", wall.at[0], wallv, 0)
    order = [0, nx - 1] + list(range(1, nx - 1))
    for i, x in enumerate(order):
        load(("coef", x), coef.at[0, :, x], cf.at[:, x], 1 + 2 * i)
        load(("source", x), source.at[0, :, x], psi0.at[:, x], 2 + 2 * i)
    load("shape", shape.at[0], tv, 1 + 2 * nx)

    started = []

    def remote(src, dst, send, recv, peer):
        copy = pltpu.make_async_remote_copy(
            src_ref=src, dst_ref=dst, send_sem=send, recv_sem=recv,
            device_id=peer, device_id_type=MESH,
        )
        copy.start()
        started.append(copy)
        return copy

    def spread(stage, slot):
        copies = []
        for d, peer in enumerate(peers[stage]):
            dst = objn.at[nd] if stage == 2 else obj.at[stage, d]
            copies.append(
                remote(own.at[stage], dst, obj_send.at[stage, d], obj_recv.at[stage, d], peer)
            )
        return copies

    def collect(stage, copies):
        total = own[stage]
        for d, copy in enumerate(copies):
            copy.wait_recv()
            total = total + obj[stage, d]
        return total

    loads["wall"].wait()
    w = wallv[...]
    width = w.shape[1]
    lane_sum = w[:, 0:LANES]
    for k in range(LANES, width, LANES):
        lane_sum = lane_sum + w[:, k:k + LANES]
    own[0] = jnp.sum(lane_sum, axis=0, keepdims=True)

    def start_psi(x, first, count):
        def step(i, carry):
            rows = pl.ds(pl.multiple_of(first + i * 8, 8), 8)
            c1, c2, c3 = cf[1, x, rows, :], cf[2, x, rows, :], cf[3, x, rows, :]
            inverse = 1.0 / (0.5 + cf[0, x, rows, :] + 2.4 * (c1 + c2 + c3))
            cf[1, x, rows, :] = c1 * inverse
            cf[2, x, rows, :] = c2 * inverse
            cf[3, x, rows, :] = c3 * inverse
            for v in range(nv):
                psi0[v, x, rows, :] = psi0[v, x, rows, :] * inverse
            return carry
        lax.fori_loop(0, count // 8, step, 0)

    def send_plane(field, halo, side, c, send, recv):
        x, peer = (nx - 1, right) if side == 0 else (0, left)
        rows = pl.ds(c * part, part)
        return remote(
            field.at[:, x, rows, :], halo.at[side, :, rows, :],
            send.at[side, c], recv.at[side, c], {"slab": peer},
        )

    pl.semaphore_wait(barrier, len(everyone))
    stage_a = spread(0, place)
    halo_copies = {}
    for x in (0, nx - 1):
        loads[("coef", x)].wait()
        loads[("source", x)].wait()
    for c in range(CHUNKS):
        for x, side in ((0, 1), (nx - 1, 0)):
            start_psi(x, c * part, part)
            halo_copies[side, c] = send_plane(psi0, halo0, side, c, send0, recv0)
    for x in range(1, nx - 1):
        loads[("coef", x)].wait()
        loads[("source", x)].wait()
        start_psi(x, 0, ny)

    own[1] = collect(0, stage_a)
    stage_b = spread(1, group)

    def stencil(field, x, v):
        p = field[v, x]
        beside_y, beside_z = shifted_pairs(p)
        if x == 0:
            beside_x = field[v, 1]
        elif x == nx - 1:
            beside_x = field[v, nx - 2]
        else:
            beside_x = field[v, x - 1] + field[v, x + 1]
        return cf[1, x] * beside_x + cf[2, x] * beside_y + cf[3, x] * beside_z

    def first_sweep(x):
        def couple(v, carry):
            mix[v] = stencil(psi0, x, v)
            return carry
        lax.fori_loop(0, nv, couple, 0)

        def combine(i, carry):
            rows = pl.ds(pl.multiple_of(i * ROWS, ROWS), ROWS)
            held = [mix[v, rows, :] for v in range(nv)]
            for o in range(nv):
                total = psi0[o, x, rows, :]
                for v in range(nv):
                    total = total + flux[0, v, o] * held[v]
                psi1[o, x, rows, :] = total
            return carry
        lax.fori_loop(0, ny // ROWS, combine, 0)

    for x in order:
        first_sweep(x)

    own[2] = collect(1, stage_b)
    objn[nd] = own[2]
    stage_c = spread(2, nd)

    has = (
        jnp.where(me > 0, 1.0, 0.0).astype(jnp.float32),
        jnp.where(me < slabs - 1, 1.0, 0.0).astype(jnp.float32),
    )
    later_copies = {}
    for c in range(CHUNKS):
        for side in (1, 0):
            came = 0 if side == 1 else 1
            x = 0 if side == 1 else nx - 1
            halo_copies[came, c].wait_recv()

            def join(i, carry):
                rows = pl.ds(pl.multiple_of(c * part + i * ROWS, ROWS), ROWS)
                held = [halo0[came, v, rows, :] for v in range(nv)]
                a = cf[1, x, rows, :] * has[came]
                for o in range(nv):
                    total = flux[0, 0, o] * held[0]
                    for v in range(1, nv):
                        total = total + flux[0, v, o] * held[v]
                    psi1[o, x, rows, :] = psi1[o, x, rows, :] + a * total
                return carry
            lax.fori_loop(0, part // ROWS, join, 0)
            later_copies[side, c] = send_plane(psi1, halo1, side, c, send1, recv1)

    loads["shape"].wait()
    for x in range(nx):
        def adjoint(i, total_sum):
            rows = pl.ds(pl.multiple_of(i * ROWS, ROWS), ROWS)
            held = [tv[v, x, rows, :] for v in range(nv)]
            product = held[0] * psi0[0, x, rows, :]
            for v in range(1, nv):
                product = product + held[v] * psi0[v, x, rows, :]
            for v in range(nv):
                total = flux[0, v, 0] * held[0]
                for o in range(1, nv):
                    total = total + flux[0, v, o] * held[o]
                tv[v, x, rows, :] = total
            return total_sum + fold_rows(product)
        acc[x] = lax.fori_loop(0, ny // ROWS, adjoint, jnp.zeros((8, nz), jnp.float32))

    for x in range(nx):
        def last_sweep(v, total):
            return total + fold_rows(tv[v, x] * stencil(psi1, x, v))
        acc[x] = lax.fori_loop(0, nv, last_sweep, acc[x])

    for copy in stage_c:
        copy.wait_recv()
    rows_of = lax.broadcasted_iota(jnp.int32, (nodes, LANES), 0)
    raw = [math.sin(math.pi * (n + 0.5) / nodes) for n in range(nodes)]
    weight = jnp.zeros((nodes, LANES), jnp.float32)
    for n in range(nodes):
        weight = jnp.where(rows_of == n, raw[n] / sum(raw), weight)
    lane_parts = jnp.zeros((nodes, LANES), jnp.float32)
    for n in range(nodes):
        lane_parts = jnp.where(rows_of == n, objn[n], lane_parts)
    objective = jnp.sum(lane_parts, axis=1, keepdims=True) * (1.0 / cells)
    mean_value = jnp.sum(weight * objective, axis=0, keepdims=True)
    variance = jnp.sum(weight * (objective - mean_value) ** 2, axis=0, keepdims=True)
    factor = weight * (1.0 + 2.0 * (objective - mean_value) / jnp.sqrt(variance + 0.25))

    for c in range(CHUNKS):
        for side in (1, 0):
            came = 0 if side == 1 else 1
            x = 0 if side == 1 else nx - 1
            later_copies[came, c].wait_recv()

            def take(i, total):
                rows = pl.ds(pl.multiple_of(c * part + i * ROWS, ROWS), ROWS)
                product = tv[0, x, rows, :] * halo1[came, 0, rows, :]
                for v in range(1, nv):
                    product = product + tv[v, x, rows, :] * halo1[came, v, rows, :]
                return total + fold_rows(cf[1, x, rows, :] * has[came] * product)
            acc[x] = lax.fori_loop(0, part // ROWS, take, acc[x])

    for x in range(nx):
        line = jnp.sum(acc[x], axis=0, keepdims=True)
        for k in range(nz // LANES):
            sens[k, x:x + 1, :] = line[:, k * LANES:(k + 1) * LANES]

    width = nz // nodes
    per_tile = LANES // width
    finals = []
    for d, peer in enumerate(peers[2]):
        finals.append(
            remote(
                sens.at[lax.div(peer["node"], per_tile)], fin.at[nd],
                fin_send.at[d], fin_recv.at[d], peer,
            )
        )
    fin[nd] = sens[lax.div(nd, per_tile)]
    for copy in finals:
        copy.wait_recv()
    total = factor[0:1, :] * fin[0]
    for n in range(1, nodes):
        total = total + factor[n:n + 1, :] * fin[n]
    column = lax.rem(nd, per_tile)
    result = total[:, 0:width]
    for k in range(1, per_tile):
        result = jnp.where(column == k, total[:, k * width:(k + 1) * width], result)
    out[...] = result
    for copy in started:
        copy.wait_send()


def solution(mesh):
    nodes, slabs = mesh.shape["node"], mesh.shape["slab"]
    inner = 2 ** (int(math.log2(slabs)) // 2)

    def per_device(source, coef, flux, shape, wall):
        _, nv, nx, ny, nz = source.shape
        f32 = jnp.float32
        dma = pltpu.SemaphoreType.DMA
        hbm = pl.BlockSpec(memory_space=pltpu.HBM)
        most = max(inner, slabs // inner, nodes) - 1
        return pl.pallas_call(
            functools.partial(kernel, nodes, slabs, inner, nx * slabs * nz),
            out_shape=jax.ShapeDtypeStruct((nx, nz // nodes), f32),
            in_specs=[hbm, hbm, pl.BlockSpec(memory_space=pltpu.SMEM), hbm, hbm],
            out_specs=pl.BlockSpec(memory_space=pltpu.VMEM),
            scratch_shapes=[
                pltpu.VMEM((nv, nx, ny, nz), f32),
                pltpu.VMEM((4, nx, ny, nz), f32),
                pltpu.VMEM((nv, nx, ny, nz), f32),
                pltpu.VMEM((nv, ny, nz), f32),
                pltpu.VMEM((nv, nx, ny, nz), f32),
                pltpu.VMEM((2, nv, ny, nz), f32),
                pltpu.VMEM((2, nv, ny, nz), f32),
                pltpu.VMEM((nx, 8, nz), f32),
                pltpu.VMEM((nx, nz), f32),
                pltpu.VMEM((2, most, 1, LANES), f32),
                pltpu.VMEM((nodes, 1, LANES), f32),
                pltpu.VMEM((3, 1, LANES), f32),
                pltpu.VMEM((nz // LANES, nx, LANES), f32),
                pltpu.VMEM((nodes, nx, LANES), f32),
                dma((2 + 2 * nx,)),
                dma((2, CHUNKS)),
                dma((2, CHUNKS)),
                dma((2, CHUNKS)),
                dma((2, CHUNKS)),
                dma((3, most)),
                dma((3, most)),
                dma((nodes - 1,)),
                dma((nodes - 1,)),
            ],
            compiler_params=pltpu.CompilerParams(
                collective_id=0, has_side_effects=True, vmem_limit_bytes=32 * 2 ** 20
            ),
        )(source, coef, flux, shape, wall)

    return jax.shard_map(
        per_device,
        mesh=mesh,
        in_specs=(
            P("node", None, "slab", None, None),
            P("node", None, "slab", None, None),
            P("node", None, None),
            P("node", None, "slab", None, None),
            P("node", "slab", None),
        ),
        out_specs=P("slab", "node"),
        check_vma=False,
    )
```

time: 263 us -> 49.7 us (0.19)
  the two profiles are of different devices: /device:TPU:8 before, /device:TPU:1 now
where the time goes in v1:
time: 49.7 us; the launch traced here: 49.5 us
  Pallas kernels  43.5 us (88%)
  local copies, waits for them, and re-layouts  5.99 us (12%)
    pallas_call x1, Pallas kernels, per_device(): pl.pallas_call(functools.partial(kernel, nodes, slabs, inner, nx * slabs...  43.5 us
    unnamed x10, local copies, waits for them, and re-layouts  5.99 us

profile of v1, /device:TPU:1, one launch (start us, length us, event | category | flops | bytes accessed | tf_op | source)
XLA Modules:
  0.0 49.5 jit_solution(13086774471816145636)
XLA Ops:
  0.0 0.7 %copy.6.flux = f32[1,6,6]{2,1,0:T(8,128)S(1)} copy(f32[1,6,6]{2,0,1:T(1,128)} %param.7) | data formatting | bytes 288 | tf_op args[2]
  0.7 0.0 copy-start
  0.7 1.4 %copy-done = f32[1,6,4,64,256]{4,3,2,1,0:T(8,128)S(1)} copy-done((f32[1,6,4,64,256]{4,3,2,1,0:T(8,128)S(1)}, f32[1,6,4,64,256]{4,3,2,1,0:T(8,128)}, u32[]{:S(2)}) %copy-start) | copy-done | bytes 1572888
  2.1 0.0 copy-start.1
  2.1 1.4 %copy-done.1 = f32[1,6,4,64,256]{4,3,2,1,0:T(8,128)S(1)} copy-done((f32[1,6,4,64,256]{4,3,2,1,0:T(8,128)S(1)}, f32[1,6,4,64,256]{4,3,2,1,0:T(8,128)}, u32[]{:S(2)}) %copy-start.1) | copy-done | bytes 1572888
  3.5 0.0 copy-start.2
  3.5 1.2 %copy-done.2 = f32[1,4,4,64,256]{4,3,2,1,0:T(8,128)S(1)} copy-done((f32[1,4,4,64,256]{4,3,2,1,0:T(8,128)S(1)}, f32[1,4,4,64,256]{4,3,2,1,0:T(8,128)}, u32[]{:S(2)}) %copy-start.2) | copy-done | bytes 1048600
  4.7 0.0 copy-start.3
  4.7 0.7 %copy-done.3 = f32[1,4,256]{2,1,0:T(4,128)S(1)} copy-done((f32[1,4,256]{2,1,0:T(4,128)S(1)}, f32[1,4,256]{2,1,0:T(4,128)}, u32[]{:S(2)}) %copy-start.3) | copy-done | bytes 4120
  5.4 43.5 %shard_map.55 = f32[4,32]{1,0:T(4,128)S(1)} custom-call(f32[1,6,4,64,256]{4,3,2,1,0:T(8,128)S(1)} %copy-done, f32[1,4,4,64,256]{4,3,2,1,0:T(8,128)S(1)} %copy-done.2, f32[1,6,6]{2,1,0:T(8,128)S(1)} %copy.6.flux, f32[1,6,4,64,256]{4,3,2,1,0:T(8,128)S(1)} %copy-done.1, f32[1,4,256]{2,1,0:T(4,128)S(1)} %copy-done.3), custom_call_target="tpu_custom_call" | custom-call | tf_op jit(solution)/shard_map/pallas_call | solution.py:292
  48.9 0.6 %copy.8 = f32[4,32]{1,0:T(4,128)} copy(f32[4,32]{1,0:T(4,128)S(1)} %shard_map.55) | data formatting | bytes 1024
Async XLA Ops:
  0.7 1.4 %copy-start = (f32[1,6,4,64,256]{4,3,2,1,0:T(8,128)S(1)}, f32[1,6,4,64,256]{4,3,2,1,0:T(8,128)}, u32[]{:S(2)}) copy-start(f32[1,6,4,64,256]{4,3,2,1,0:T(8,128)} %source.1) | copy-start | bytes 4718596
  2.1 1.4 %copy-start.1 = (f32[1,6,4,64,256]{4,3,2,1,0:T(8,128)S(1)}, f32[1,6,4,64,256]{4,3,2,1,0:T(8,128)}, u32[]{:S(2)}) copy-start(f32[1,6,4,64,256]{4,3,2,1,0:T(8,128)} %shape.1) | copy-start | bytes 4718596
  3.5 1.2 %copy-start.2 = (f32[1,4,4,64,256]{4,3,2,1,0:T(8,128)S(1)}, f32[1,4,4,64,256]{4,3,2,1,0:T(8,128)}, u32[]{:S(2)}) copy-start(f32[1,4,4,64,256]{4,3,2,1,0:T(8,128)} %coef.1) | copy-start | bytes 3145732
  4.7 0.7 %copy-start.3 = (f32[1,4,256]{2,1,0:T(4,128)S(1)}, f32[1,4,256]{2,1,0:T(4,128)}, u32[]{:S(2)}) copy-start(f32[1,4,256]{2,1,0:T(4,128)} %wall.1) | copy-start | bytes 12292

commit v2 on v1

--- a/solution.py
+++ b/solution.py
@@ -31,8 +31,8 @@
 
 def kernel(
     nodes, slabs, inner, cells,
-    source, coef, flux, shape, wall, out,
-    psi0, cf, psi1, mix, tv, halo0, halo1, acc, wallv, obj, objn, own, sens, fin,
+    source, coef, flux_in, shape, wall, out,
+    flux, psi0, cf, psi1, mix, tv, halo0, halo1, acc, wallv, obj, objn, own, sens, fin,
     load_sem, send0, recv0, send1, recv1, obj_send, obj_recv, fin_send, fin_recv,
 ):
     me, nd = lax.axis_index("slab"), lax.axis_index("node")
@@ -64,7 +64,8 @@
     for i, x in enumerate(order):
         load(("coef", x), coef.at[0, :, x], cf.at[:, x], 1 + 2 * i)
         load(("source", x), source.at[0, :, x], psi0.at[:, x], 2 + 2 * i)
-    load("shape", shape.at[0], tv, 1 + 2 * nx)
+    load("flux", flux_in, flux, 1 + 2 * nx)
+    load("shape", shape.at[0], tv, 2 + 2 * nx)
 
     started = []
 
@@ -163,11 +164,12 @@
             for o in range(nv):
                 total = psi0[o, x, rows, :]
                 for v in range(nv):
-                    total = total + flux[0, v, o] * held[v]
+                    total = total + flux[v, 0, o] * held[v]
                 psi1[o, x, rows, :] = total
             return carry
         lax.fori_loop(0, ny // ROWS, combine, 0)
 
+    loads["flux"].wait()
     for x in order:
         first_sweep(x)
 
@@ -193,7 +195,7 @@
                 for o in range(nv):
                     total = flux[0, 0, o] * held[0]
                     for v in range(1, nv):
-                        total = total + flux[0, v, o] * held[v]
+                        total = total + flux[v, 0, o] * held[v]
                     psi1[o, x, rows, :] = psi1[o, x, rows, :] + a * total
                 return carry
             lax.fori_loop(0, part // ROWS, join, 0)
@@ -208,9 +210,9 @@
             for v in range(1, nv):
                 product = product + held[v] * psi0[v, x, rows, :]
             for v in range(nv):
-                total = flux[0, v, 0] * held[0]
+                total = flux[v, 0, 0] * held[0]
                 for o in range(1, nv):
-                    total = total + flux[0, v, o] * held[o]
+                    total = total + flux[v, 0, o] * held[o]
                 tv[v, x, rows, :] = total
             return total_sum + fold_rows(product)
         acc[x] = lax.fori_loop(0, ny // ROWS, adjoint, jnp.zeros((8, nz), jnp.float32))
@@ -292,9 +294,10 @@
         return pl.pallas_call(
             functools.partial(kernel, nodes, slabs, inner, nx * slabs * nz),
             out_shape=jax.ShapeDtypeStruct((nx, nz // nodes), f32),
-            in_specs=[hbm, hbm, pl.BlockSpec(memory_space=pltpu.SMEM), hbm, hbm],
+            in_specs=[hbm, hbm, hbm, hbm, hbm],
             out_specs=pl.BlockSpec(memory_space=pltpu.VMEM),
             scratch_shapes=[
+                pltpu.SMEM((nv, 1, nv), f32),
                 pltpu.VMEM((nv, nx, ny, nz), f32),
                 pltpu.VMEM((4, nx, ny, nz), f32),
                 pltpu.VMEM((nv, nx, ny, nz), f32),
@@ -309,7 +312,7 @@
                 pltpu.VMEM((3, 1, LANES), f32),
                 pltpu.VMEM((nz // LANES, nx, LANES), f32),
                 pltpu.VMEM((nodes, nx, LANES), f32),
-                dma((2 + 2 * nx,)),
+                dma((3 + 2 * nx,)),
                 dma((2, CHUNKS)),
                 dma((2, CHUNKS)),
                 dma((2, CHUNKS)),
@@ -320,9 +323,9 @@
                 dma((nodes - 1,)),
             ],
             compiler_params=pltpu.CompilerParams(
-                collective_id=0, has_side_effects=True, vmem_limit_bytes=32 * 2 ** 20
+                collective_id=0, has_side_effects=True, vmem_limit_bytes=60 * 2 ** 20
             ),
-        )(source, coef, flux, shape, wall)
+        )(source, coef, jnp.transpose(flux, (1, 0, 2)), shape, wall)
 
     return jax.shard_map(
         per_device,

time: 49.7 us -> 44.9 us (0.903)
  local copies, waits for them, and re-layouts: 5.99 us -> 1.26 us
    unnamed x10 -> x1, local copies, waits for them, and re-layouts: 5.99 us -> 1.26 us
where the time goes in v2:
time: 44.9 us; the launch traced here: 44.7 us
  Pallas kernels  43.5 us (97%)
  local copies, waits for them, and re-layouts  1.26 us (3%)
    pallas_call x1, Pallas kernels, per_device(): pl.pallas_call(functools.partial(kernel, nodes, slabs, inner, nx * slabs...  43.5 us
    unnamed x1, local copies, waits for them, and re-layouts  1.26 us

profile of v2, /device:TPU:1, one launch (start us, length us, event | category | flops | bytes accessed | tf_op | source)
XLA Modules:
  0.0 44.7 jit_solution(2683534992769494550)
XLA Ops:
  0.0 43.5 %shard_map.55 = f32[4,32]{1,0:T(4,128)} custom-call(f32[1,6,4,64,256]{4,3,2,1,0:T(8,128)} %source.1, f32[1,4,4,64,256]{4,3,2,1,0:T(8,128)} %coef.1, f32[6,1,6]{2,1,0:T(1,128)} %bitcast.1, f32[1,6,4,64,256]{4,3,2,1,0:T(8,128)} %shape.1, f32[1,4,256]{2,1,0:T(4,128)} %wall.1), custom_call_target="tpu_custom_call" | custom-call | tf_op jit(solution)/shard_map/pallas_call | solution.py:294
  43.5 1.3 %copy.7 = f32[4,32]{1,0:T(4,128)} copy(f32[4,32]{1,0:T(4,128)} %shard_map.55) | data formatting | bytes 1024

commit v3 on v2

--- a/solution.py
+++ b/solution.py
@@ -9,7 +9,7 @@
 from jax.sharding import PartitionSpec as P
 
 MESH = pl.DeviceIdType.MESH
-CHUNKS = 2
+CHUNKS = 4
 ROWS = 16
 LANES = 128
 
@@ -38,7 +38,8 @@
     me, nd = lax.axis_index("slab"), lax.axis_index("node")
     outer = slabs // inner
     place, group = lax.rem(me, inner), lax.div(me, inner)
-    right, left = lax.rem(me + 1, slabs), lax.rem(me + slabs - 1, slabs)
+    has_left, has_right = me > 0, me < slabs - 1
+    left, right = {"slab": me - 1}, {"slab": me + 1}
     nv, nx, ny, nz = psi0.shape
     part = ny // CHUNKS
 
@@ -49,9 +50,16 @@
     ]
 
     barrier = pltpu.get_barrier_semaphore()
-    everyone = [{"slab": left}, {"slab": right}] + peers[0] + peers[1] + peers[2]
+
+    def greet(peer):
+        pl.semaphore_signal(barrier, inc=1, device_id=peer, device_id_type=MESH)
+
+    pl.when(has_left & (place == 0))(lambda: greet(left))
+    pl.when(has_right & (place == inner - 1))(lambda: greet(right))
+    everyone = peers[0] + peers[1] + peers[2]
     for peer in everyone:
-        pl.semaphore_signal(barrier, inc=1, device_id=peer, device_id_type=MESH)
+        greet(peer)
+    beyond = jnp.where(has_left & (place == 0), 1, 0) + jnp.where(has_right & (place == inner - 1), 1, 0)
 
     loads = {}
 
@@ -75,7 +83,6 @@
             device_id=peer, device_id_type=MESH,
         )
         copy.start()
-        started.append(copy)
         return copy
 
     def spread(stage, slot):
@@ -85,6 +92,7 @@
             copies.append(
                 remote(own.at[stage], dst, obj_send.at[stage, d], obj_recv.at[stage, d], peer)
             )
+        started.extend(copies)
         return copies
 
     def collect(stage, copies):
@@ -115,31 +123,30 @@
             return carry
         lax.fori_loop(0, count // 8, step, 0)
 
-    def send_plane(field, halo, side, c, send, recv):
+    def plane_copy(field, halo, side, c, send, recv):
         x, peer = (nx - 1, right) if side == 0 else (0, left)
         rows = pl.ds(c * part, part)
-        return remote(
-            field.at[:, x, rows, :], halo.at[side, :, rows, :],
-            send.at[side, c], recv.at[side, c], {"slab": peer},
+        return pltpu.make_async_remote_copy(
+            src_ref=field.at[:, x, rows, :], dst_ref=halo.at[side, :, rows, :],
+            send_sem=send.at[side, c], recv_sem=recv.at[side, c],
+            device_id=peer, device_id_type=MESH,
         )
 
-    pl.semaphore_wait(barrier, len(everyone))
-    stage_a = spread(0, place)
-    halo_copies = {}
+    sides = ((0, 1, 0, has_left), (1, 0, nx - 1, has_right))
+
+    pl.semaphore_wait(barrier, len(everyone) + beyond)
     for x in (0, nx - 1):
         loads[("coef", x)].wait()
         loads[("source", x)].wait()
+    stage_a = spread(0, place)
     for c in range(CHUNKS):
-        for x, side in ((0, 1), (nx - 1, 0)):
+        for came, goes, x, there in sides:
             start_psi(x, c * part, part)
-            halo_copies[side, c] = send_plane(psi0, halo0, side, c, send0, recv0)
+            pl.when(there)(plane_copy(psi0, halo0, goes, c, send0, recv0).start)
     for x in range(1, nx - 1):
         loads[("coef", x)].wait()
         loads[("source", x)].wait()
         start_psi(x, 0, ny)
-
-    own[1] = collect(0, stage_a)
-    stage_b = spread(1, group)
 
     def stencil(field, x, v):
         p = field[v, x]
@@ -173,33 +180,28 @@
     for x in order:
         first_sweep(x)
 
-    own[2] = collect(1, stage_b)
-    objn[nd] = own[2]
-    stage_c = spread(2, nd)
-
-    has = (
-        jnp.where(me > 0, 1.0, 0.0).astype(jnp.float32),
-        jnp.where(me < slabs - 1, 1.0, 0.0).astype(jnp.float32),
-    )
-    later_copies = {}
+    own[1] = collect(0, stage_a)
+    stage_b = spread(1, group)
+
+    def join(came, goes, x, c):
+        plane_copy(psi0, halo0, came, c, send0, recv0).wait_recv()
+
+        def step(i, carry):
+            rows = pl.ds(pl.multiple_of(c * part + i * ROWS, ROWS), ROWS)
+            held = [halo0[came, v, rows, :] for v in range(nv)]
+            a = cf[1, x, rows, :]
+            for o in range(nv):
+                total = flux[0, 0, o] * held[0]
+                for v in range(1, nv):
+                    total = total + flux[v, 0, o] * held[v]
+                psi1[o, x, rows, :] = psi1[o, x, rows, :] + a * total
+            return carry
+        lax.fori_loop(0, part // ROWS, step, 0)
+        plane_copy(psi1, halo1, goes, c, send1, recv1).start()
+
     for c in range(CHUNKS):
-        for side in (1, 0):
-            came = 0 if side == 1 else 1
-            x = 0 if side == 1 else nx - 1
-            halo_copies[came, c].wait_recv()
-
-            def join(i, carry):
-                rows = pl.ds(pl.multiple_of(c * part + i * ROWS, ROWS), ROWS)
-                held = [halo0[came, v, rows, :] for v in range(nv)]
-                a = cf[1, x, rows, :] * has[came]
-                for o in range(nv):
-                    total = flux[0, 0, o] * held[0]
-                    for v in range(1, nv):
-                        total = total + flux[v, 0, o] * held[v]
-                    psi1[o, x, rows, :] = psi1[o, x, rows, :] + a * total
-                return carry
-            lax.fori_loop(0, part // ROWS, join, 0)
-            later_copies[side, c] = send_plane(psi1, halo1, side, c, send1, recv1)
+        for came, goes, x, there in sides:
+            pl.when(there)(functools.partial(join, came, goes, x, c))
 
     loads["shape"].wait()
     for x in range(nx):
@@ -217,6 +219,10 @@
             return total_sum + fold_rows(product)
         acc[x] = lax.fori_loop(0, ny // ROWS, adjoint, jnp.zeros((8, nz), jnp.float32))
 
+    own[2] = collect(1, stage_b)
+    objn[nd] = own[2]
+    stage_c = spread(2, nd)
+
     for x in range(nx):
         def last_sweep(v, total):
             return total + fold_rows(tv[v, x] * stencil(psi1, x, v))
@@ -237,19 +243,20 @@
     variance = jnp.sum(weight * (objective - mean_value) ** 2, axis=0, keepdims=True)
     factor = weight * (1.0 + 2.0 * (objective - mean_value) / jnp.sqrt(variance + 0.25))
 
+    def take(came, x, c):
+        plane_copy(psi1, halo1, came, c, send1, recv1).wait_recv()
+
+        def step(i, total):
+            rows = pl.ds(pl.multiple_of(c * part + i * ROWS, ROWS), ROWS)
+            product = tv[0, x, rows, :] * halo1[came, 0, rows, :]
+            for v in range(1, nv):
+                product = product + tv[v, x, rows, :] * halo1[came, v, rows, :]
+            return total + fold_rows(cf[1, x, rows, :] * product)
+        acc[x] = lax.fori_loop(0, part // ROWS, step, acc[x])
+
     for c in range(CHUNKS):
-        for side in (1, 0):
-            came = 0 if side == 1 else 1
-            x = 0 if side == 1 else nx - 1
-            later_copies[came, c].wait_recv()
-
-            def take(i, total):
-                rows = pl.ds(pl.multiple_of(c * part + i * ROWS, ROWS), ROWS)
-                product = tv[0, x, rows, :] * halo1[came, 0, rows, :]
-                for v in range(1, nv):
-                    product = product + tv[v, x, rows, :] * halo1[came, v, rows, :]
-                return total + fold_rows(cf[1, x, rows, :] * has[came] * product)
-            acc[x] = lax.fori_loop(0, part // ROWS, take, acc[x])
+        for came, goes, x, there in sides:
+            pl.when(there)(functools.partial(take, came, x, c))
 
     for x in range(nx):
         line = jnp.sum(acc[x], axis=0, keepdims=True)
@@ -277,8 +284,12 @@
     for k in range(1, per_tile):
         result = jnp.where(column == k, total[:, k * width:(k + 1) * width], result)
     out[...] = result
-    for copy in started:
+    for copy in started + finals:
         copy.wait_send()
+    for c in range(CHUNKS):
+        for came, goes, x, there in sides:
+            pl.when(there)(plane_copy(psi0, halo0, goes, c, send0, recv0).wait_send)
+            pl.when(there)(plane_copy(psi1, halo1, goes, c, send1, recv1).wait_send)
 
 
 def solution(mesh):

time: 44.9 us -> 42 us (0.935)
  the two profiles are of different devices: /device:TPU:1 before, /device:TPU:41 now
where the time goes in v3:
time: 42 us; the launch traced here: 41.9 us
  Pallas kernels  40.6 us (97%)
  local copies, waits for them, and re-layouts  1.26 us (3%)
    pallas_call x1, Pallas kernels, per_device(): pl.pallas_call(functools.partial(kernel, nodes, slabs, inner, nx * slabs...  40.6 us
    unnamed x1, local copies, waits for them, and re-layouts  1.26 us

profile of v3, /device:TPU:41, one launch (start us, length us, event | category | flops | bytes accessed | tf_op | source)
XLA Modules:
  0.0 41.9 jit_solution(12020776744168027989)
XLA Ops:
  0.0 40.6 %shard_map.55 = f32[4,32]{1,0:T(4,128)} custom-call(f32[1,6,4,64,256]{4,3,2,1,0:T(8,128)} %source.1, f32[1,4,4,64,256]{4,3,2,1,0:T(8,128)} %coef.1, f32[6,1,6]{2,1,0:T(1,128)} %bitcast.1, f32[1,6,4,64,256]{4,3,2,1,0:T(8,128)} %shape.1, f32[1,4,256]{2,1,0:T(4,128)} %wall.1), custom_call_target="tpu_custom_call" | custom-call | tf_op jit(solution)/shard_map/pallas_call | solution.py:305
  40.6 1.3 %copy.7 = f32[4,32]{1,0:T(4,128)} copy(f32[4,32]{1,0:T(4,128)} %shard_map.55) | data formatting | bytes 1024

commit v4 on v3

--- a/solution.py
+++ b/solution.py
@@ -10,6 +10,9 @@
 
 MESH = pl.DeviceIdType.MESH
 CHUNKS = 4
+TURNED = 2
+DEFERRED = 2
+ANSWER = (0, 0)
 ROWS = 16
 LANES = 128
 
@@ -32,8 +35,8 @@
 def kernel(
     nodes, slabs, inner, cells,
     source, coef, flux_in, shape, wall, out,
-    flux, psi0, cf, psi1, mix, tv, halo0, halo1, acc, wallv, obj, objn, own, sens, fin,
-    load_sem, send0, recv0, send1, recv1, obj_send, obj_recv, fin_send, fin_recv,
+    flux, psi0, cf, psi1, mix, tv, halo0, halo1, gsend, gheld, rsend, rheld, plain, aheld, acc, wallv, obj, own, sens, fin,
+    load_sem, turn_send, turn_recv, send0, recv0, send1, recv1, obj_send, obj_recv, fin_send, fin_recv,
 ):
     me, nd = lax.axis_index("slab"), lax.axis_index("node")
     outer = slabs // inner
@@ -63,17 +66,24 @@
 
     loads = {}
 
-    def load(name, src, dst, index):
-        loads[name] = pltpu.make_async_copy(src, dst, load_sem.at[index])
+    def load(name, src, dst):
+        loads[name] = pltpu.make_async_copy(src, dst, load_sem.at[len(loads)])
         loads[name].start()
 
-    load("wall", wall.at[0], wallv, 0)
+    load("wall", wall.at[0], wallv)
+    cuts = ((0, part), (part, ny - part))
+    for k, (first, count) in enumerate(cuts):
+        rows = pl.ds(first, count)
+        for x in (0, nx - 1):
+            load(("coef", x, k), coef.at[0, :, x, rows, :], cf.at[:, x, rows, :])
+            load(("source", x, k), source.at[0, :, x, rows, :], psi0.at[:, x, rows, :])
+
+    middle = pl.ds(1, nx - 2)
+    load("coef", coef.at[0, :, middle], cf.at[:, middle])
+    load("source", source.at[0, :, middle], psi0.at[:, middle])
+    load("flux", flux_in, flux)
+    load("shape", shape.at[0], tv)
     order = [0, nx - 1] + list(range(1, nx - 1))
-    for i, x in enumerate(order):
-        load(("coef", x), coef.at[0, :, x], cf.at[:, x], 1 + 2 * i)
-        load(("source", x), source.at[0, :, x], psi0.at[:, x], 2 + 2 * i)
-    load("flux", flux_in, flux, 1 + 2 * nx)
-    load("shape", shape.at[0], tv, 2 + 2 * nx)
 
     started = []
 
@@ -88,9 +98,8 @@
     def spread(stage, slot):
         copies = []
         for d, peer in enumerate(peers[stage]):
-            dst = objn.at[nd] if stage == 2 else obj.at[stage, d]
             copies.append(
-                remote(own.at[stage], dst, obj_send.at[stage, d], obj_recv.at[stage, d], peer)
+                remote(own.at[stage], obj.at[stage, d], obj_send.at[stage, d], obj_recv.at[stage, d], peer)
             )
         started.extend(copies)
         return copies
@@ -134,18 +143,67 @@
 
     sides = ((0, 1, 0, has_left), (1, 0, nx - 1, has_right))
 
+    ends_row, opens_row = has_right & (place == inner - 1), has_left & (place == 0)
+    to_left = pltpu.make_async_remote_copy(
+        src_ref=gsend, dst_ref=gheld, send_sem=turn_send.at[0], recv_sem=turn_recv.at[0],
+        device_id=left, device_id_type=MESH,
+    )
+    to_right = pltpu.make_async_remote_copy(
+        src_ref=rsend, dst_ref=rheld, send_sem=turn_send.at[1], recv_sem=turn_recv.at[1],
+        device_id=right, device_id_type=MESH,
+    )
+
+    coupling = pltpu.make_async_remote_copy(
+        src_ref=cf.at[1, nx - 1], dst_ref=aheld, send_sem=turn_send.at[2],
+        recv_sem=turn_recv.at[2], device_id=right, device_id_type=MESH,
+    )
+
+    def plain_copy(c):
+        rows = pl.ds(c * part, part)
+        return pltpu.make_async_remote_copy(
+            src_ref=plain.at[:, rows, :], dst_ref=halo1.at[0, :, rows, :],
+            send_sem=send1.at[0, c], recv_sem=recv1.at[0, c],
+            device_id=right, device_id_type=MESH,
+        )
+
+    def send_plain():
+        plain[...] = psi1[:, nx - 1]
+        for c in range(TURNED, CHUNKS):
+            plain_copy(c).start()
+
+    def turn():
+        def step(i, carry):
+            rows = pl.ds(pl.multiple_of(i * ROWS, ROWS), ROWS)
+            a = cf[1, 0, rows, :]
+            held = [tv[v, 0, rows, :] for v in range(nv)]
+            for v in range(nv):
+                total = flux[v, 0, 0] * held[0]
+                for o in range(1, nv):
+                    total = total + flux[v, 0, o] * held[o]
+                gsend[v, rows, :] = a * total
+            return carry
+        lax.fori_loop(0, TURNED * part // ROWS, step, 0)
+
+    for k in range(len(cuts)):
+        for x in (0, nx - 1):
+            loads["coef", x, k].wait()
+            loads["source", x, k].wait()
+    for x in (0, nx - 1):
+        start_psi(x, 0, ny)
+    loads["flux"].wait()
+    loads["shape"].wait()
+    pl.when(opens_row)(turn)
+
     pl.semaphore_wait(barrier, len(everyone) + beyond)
-    for x in (0, nx - 1):
-        loads[("coef", x)].wait()
-        loads[("source", x)].wait()
     stage_a = spread(0, place)
+    pl.when(opens_row)(to_left.start)
     for c in range(CHUNKS):
         for came, goes, x, there in sides:
-            start_psi(x, c * part, part)
             pl.when(there)(plane_copy(psi0, halo0, goes, c, send0, recv0).start)
+    pl.when(ends_row)(coupling.start)
+    loads["coef"].wait()
+    loads["source"].wait()
     for x in range(1, nx - 1):
-        loads[("coef", x)].wait()
-        loads[("source", x)].wait()
         start_psi(x, 0, ny)
 
     def stencil(field, x, v):
@@ -176,34 +234,10 @@
             return carry
         lax.fori_loop(0, ny // ROWS, combine, 0)
 
-    loads["flux"].wait()
     for x in order:
         first_sweep(x)
-
-    own[1] = collect(0, stage_a)
-    stage_b = spread(1, group)
-
-    def join(came, goes, x, c):
-        plane_copy(psi0, halo0, came, c, send0, recv0).wait_recv()
-
-        def step(i, carry):
-            rows = pl.ds(pl.multiple_of(c * part + i * ROWS, ROWS), ROWS)
-            held = [halo0[came, v, rows, :] for v in range(nv)]
-            a = cf[1, x, rows, :]
-            for o in range(nv):
-                total = flux[0, 0, o] * held[0]
-                for v in range(1, nv):
-                    total = total + flux[v, 0, o] * held[v]
-                psi1[o, x, rows, :] = psi1[o, x, rows, :] + a * total
-            return carry
-        lax.fori_loop(0, part // ROWS, step, 0)
-        plane_copy(psi1, halo1, goes, c, send1, recv1).start()
-
-    for c in range(CHUNKS):
-        for came, goes, x, there in sides:
-            pl.when(there)(functools.partial(join, came, goes, x, c))
-
-    loads["shape"].wait()
+    pl.when(ends_row)(send_plain)
+
     for x in range(nx):
         def adjoint(i, total_sum):
             rows = pl.ds(pl.multiple_of(i * ROWS, ROWS), ROWS)
@@ -219,29 +253,55 @@
             return total_sum + fold_rows(product)
         acc[x] = lax.fori_loop(0, ny // ROWS, adjoint, jnp.zeros((8, nz), jnp.float32))
 
-    own[2] = collect(1, stage_b)
-    objn[nd] = own[2]
-    stage_c = spread(2, nd)
+    own[1] = collect(0, stage_a)
+    stage_b = spread(1, group)
+
+    def join(came, goes, x, c):
+        plane_copy(psi0, halo0, came, c, send0, recv0).wait_recv()
+
+        def step(i, carry):
+            rows = pl.ds(pl.multiple_of(c * part + i * ROWS, ROWS), ROWS)
+            held = [halo0[came, v, rows, :] for v in range(nv)]
+            a = cf[1, x, rows, :]
+            for o in range(nv):
+                total = flux[0, 0, o] * held[0]
+                for v in range(1, nv):
+                    total = total + flux[v, 0, o] * held[v]
+                psi1[o, x, rows, :] = psi1[o, x, rows, :] + a * total
+            return carry
+        lax.fori_loop(0, part // ROWS, step, 0)
+        follow = plane_copy(psi1, halo1, goes, c, send1, recv1)
+        if goes == 0:
+            pl.when(jnp.logical_not(ends_row))(follow.start)
+        elif c >= CHUNKS - DEFERRED:
+            pl.when(jnp.logical_not(opens_row))(follow.start)
+        else:
+            follow.start()
+
+    def answer():
+        to_left.wait_recv()
+
+        def step(i, total):
+            rows = pl.ds(pl.multiple_of(i * ROWS, ROWS), ROWS)
+            product = gheld[0, rows, :] * plain[0, rows, :]
+            for v in range(1, nv):
+                product = product + gheld[v, rows, :] * plain[v, rows, :]
+            return total + fold_rows(product)
+        rsend[...] = lax.fori_loop(
+            0, TURNED * part // ROWS, step, jnp.zeros((8, nz), jnp.float32)
+        )
+        to_right.start()
+
+    for c in range(CHUNKS):
+        for came, goes, x, there in sides:
+            pl.when(there)(functools.partial(join, came, goes, x, c))
+            if (came, c) == ANSWER:
+                pl.when(ends_row)(answer)
 
     for x in range(nx):
         def last_sweep(v, total):
             return total + fold_rows(tv[v, x] * stencil(psi1, x, v))
         acc[x] = lax.fori_loop(0, nv, last_sweep, acc[x])
-
-    for copy in stage_c:
-        copy.wait_recv()
-    rows_of = lax.broadcasted_iota(jnp.int32, (nodes, LANES), 0)
-    raw = [math.sin(math.pi * (n + 0.5) / nodes) for n in range(nodes)]
-    weight = jnp.zeros((nodes, LANES), jnp.float32)
-    for n in range(nodes):
-        weight = jnp.where(rows_of == n, raw[n] / sum(raw), weight)
-    lane_parts = jnp.zeros((nodes, LANES), jnp.float32)
-    for n in range(nodes):
-        lane_parts = jnp.where(rows_of == n, objn[n], lane_parts)
-    objective = jnp.sum(lane_parts, axis=1, keepdims=True) * (1.0 / cells)
-    mean_value = jnp.sum(weight * objective, axis=0, keepdims=True)
-    variance = jnp.sum(weight * (objective - mean_value) ** 2, axis=0, keepdims=True)
-    factor = weight * (1.0 + 2.0 * (objective - mean_value) / jnp.sqrt(variance + 0.25))
 
     def take(came, x, c):
         plane_copy(psi1, halo1, came, c, send1, recv1).wait_recv()
@@ -254,14 +314,38 @@
             return total + fold_rows(cf[1, x, rows, :] * product)
         acc[x] = lax.fori_loop(0, part // ROWS, step, acc[x])
 
+    def add_answer():
+        coupling.wait_recv()
+
+        def step(i, total):
+            rows = pl.ds(pl.multiple_of(i * ROWS, ROWS), ROWS)
+            held = [psi0[v, 0, rows, :] for v in range(nv)]
+            product = jnp.zeros((ROWS, nz), jnp.float32)
+            for o in range(nv):
+                mixed = flux[0, 0, o] * held[0]
+                for v in range(1, nv):
+                    mixed = mixed + flux[v, 0, o] * held[v]
+                product = product + tv[o, 0, rows, :] * mixed
+            return total + fold_rows(aheld[rows, :] * cf[1, 0, rows, :] * product)
+        added = lax.fori_loop(0, ny // ROWS, step, acc[0])
+        to_right.wait_recv()
+        acc[0] = added + rheld[...]
+
     for c in range(CHUNKS):
         for came, goes, x, there in sides:
+            if came == 0 and c < TURNED:
+                there = there & jnp.logical_not(opens_row)
             pl.when(there)(functools.partial(take, came, x, c))
+    pl.when(opens_row)(add_answer)
 
     for x in range(nx):
         line = jnp.sum(acc[x], axis=0, keepdims=True)
         for k in range(nz // LANES):
             sens[k, x:x + 1, :] = line[:, k * LANES:(k + 1) * LANES]
+
+    objective_part = collect(1, stage_b)
+    for k in range(nz // LANES):
+        sens[k, nx:8, :] = jnp.broadcast_to(objective_part, (8 - nx, LANES))
 
     width = nz // nodes
     per_tile = LANES // width
@@ -273,12 +357,27 @@
                 fin_send.at[d], fin_recv.at[d], peer,
             )
         )
+    for c in range(CHUNKS - DEFERRED, CHUNKS):
+        pl.when(opens_row)(plane_copy(psi1, halo1, 1, c, send1, recv1).start)
     fin[nd] = sens[lax.div(nd, per_tile)]
     for copy in finals:
         copy.wait_recv()
-    total = factor[0:1, :] * fin[0]
+    rows_of = lax.broadcasted_iota(jnp.int32, (nodes, LANES), 0)
+    raw = [math.sin(math.pi * (n + 0.5) / nodes) for n in range(nodes)]
+    weight = jnp.zeros((nodes, LANES), jnp.float32)
+    for n in range(nodes):
+        weight = jnp.where(rows_of == n, raw[n] / sum(raw), weight)
+    lane_parts = jnp.zeros((nodes, LANES), jnp.float32)
+    for n in range(nodes):
+        lane_parts = jnp.where(rows_of == n, fin[n, nx:nx + 1, :], lane_parts)
+    objective = jnp.sum(lane_parts, axis=1, keepdims=True) * (1.0 / cells)
+    mean_value = jnp.sum(weight * objective, axis=0, keepdims=True)
+    variance = jnp.sum(weight * (objective - mean_value) ** 2, axis=0, keepdims=True)
+    factor = weight * (1.0 + 2.0 * (objective - mean_value) / jnp.sqrt(variance + 0.25))
+
+    total = factor[0:1, :] * fin[0, 0:nx, :]
     for n in range(1, nodes):
-        total = total + factor[n:n + 1, :] * fin[n]
+        total = total + factor[n:n + 1, :] * fin[n, 0:nx, :]
     column = lax.rem(nd, per_tile)
     result = total[:, 0:width]
     for k in range(1, per_tile):
@@ -289,7 +388,14 @@
     for c in range(CHUNKS):
         for came, goes, x, there in sides:
             pl.when(there)(plane_copy(psi0, halo0, goes, c, send0, recv0).wait_send)
+            if goes == 0:
+                there = there & jnp.logical_not(ends_row)
             pl.when(there)(plane_copy(psi1, halo1, goes, c, send1, recv1).wait_send)
+        if c >= TURNED:
+            pl.when(ends_row)(plain_copy(c).wait_send)
+    pl.when(ends_row)(coupling.wait_send)
+    pl.when(opens_row)(to_left.wait_send)
+    pl.when(ends_row)(to_right.wait_send)
 
 
 def solution(mesh):
@@ -316,20 +422,27 @@
                 pltpu.VMEM((nv, nx, ny, nz), f32),
                 pltpu.VMEM((2, nv, ny, nz), f32),
                 pltpu.VMEM((2, nv, ny, nz), f32),
+                pltpu.VMEM((nv, ny * TURNED // CHUNKS, nz), f32),
+                pltpu.VMEM((nv, ny * TURNED // CHUNKS, nz), f32),
+                pltpu.VMEM((8, nz), f32),
+                pltpu.VMEM((8, nz), f32),
+                pltpu.VMEM((nv, ny, nz), f32),
+                pltpu.VMEM((ny, nz), f32),
                 pltpu.VMEM((nx, 8, nz), f32),
                 pltpu.VMEM((nx, nz), f32),
                 pltpu.VMEM((2, most, 1, LANES), f32),
-                pltpu.VMEM((nodes, 1, LANES), f32),
-                pltpu.VMEM((3, 1, LANES), f32),
-                pltpu.VMEM((nz // LANES, nx, LANES), f32),
-                pltpu.VMEM((nodes, nx, LANES), f32),
-                dma((3 + 2 * nx,)),
+                pltpu.VMEM((2, 1, LANES), f32),
+                pltpu.VMEM((nz // LANES, 8, LANES), f32),
+                pltpu.VMEM((nodes, 8, LANES), f32),
+                dma((13,)),
+                dma((3,)),
+                dma((3,)),
                 dma((2, CHUNKS)),
                 dma((2, CHUNKS)),
                 dma((2, CHUNKS)),
                 dma((2, CHUNKS)),
-                dma((3, most)),
-                dma((3, most)),
+                dma((2, most)),
+                dma((2, most)),
                 dma((nodes - 1,)),
                 dma((nodes - 1,)),
             ],

time: 42 us -> 40.8 us (0.971)
  the two profiles are of different devices: /device:TPU:41 before, /device:TPU:1 now
where the time goes in v4:
time: 40.8 us; the launch traced here: 40.4 us
  Pallas kernels  39.1 us (96%)
  local copies, waits for them, and re-layouts  1.26 us (3%)
    pallas_call x1, Pallas kernels, per_device(): pl.pallas_call(functools.partial(kernel, nodes, slabs, inner, nx * slabs...  39.1 us
    unnamed x1, local copies, waits for them, and re-layouts  1.26 us

profile of v4, /device:TPU:1, one launch (start us, length us, event | category | flops | bytes accessed | tf_op | source)
XLA Modules:
  0.0 40.4 jit_solution(3942110532076450225)
XLA Ops:
  0.0 39.1 %shard_map.55 = f32[4,32]{1,0:T(4,128)} custom-call(f32[1,6,4,64,256]{4,3,2,1,0:T(8,128)} %source.1, f32[1,4,4,64,256]{4,3,2,1,0:T(8,128)} %coef.1, f32[6,1,6]{2,1,0:T(1,128)} %bitcast.1, f32[1,6,4,64,256]{4,3,2,1,0:T(8,128)} %shape.1, f32[1,4,256]{2,1,0:T(4,128)} %wall.1), custom_call_target="tpu_custom_call" | custom-call | tf_op jit(solution)/shard_map/pallas_call | solution.py:411
  39.2 1.3 %copy.7 = f32[4,32]{1,0:T(4,128)} copy(f32[4,32]{1,0:T(4,128)} %shard_map.55) | data formatting | bytes 1024

commit v5 on v4

--- a/solution.py
+++ b/solution.py
@@ -195,11 +195,12 @@
     pl.when(opens_row)(turn)
 
     pl.semaphore_wait(barrier, len(everyone) + beyond)
-    stage_a = spread(0, place)
     pl.when(opens_row)(to_left.start)
     for c in range(CHUNKS):
         for came, goes, x, there in sides:
             pl.when(there)(plane_copy(psi0, halo0, goes, c, send0, recv0).start)
+        if c == 0:
+            stage_a = spread(0, place)
     pl.when(ends_row)(coupling.start)
     loads["coef"].wait()
     loads["source"].wait()
@@ -447,7 +448,7 @@
                 dma((nodes - 1,)),
             ],
             compiler_params=pltpu.CompilerParams(
-                collective_id=0, has_side_effects=True, vmem_limit_bytes=60 * 2 ** 20
+                collective_id=0, has_side_effects=True, vmem_limit_bytes=56551424
             ),
         )(source, coef, jnp.transpose(flux, (1, 0, 2)), shape, wall)
 

time: 40.8 us -> 39.5 us (0.968)
  local copies, waits for them, and re-layouts: 1.26 us -> 0.58 us
  Pallas kernels: 39.1 us -> 38.6 us
    unnamed x1, local copies, waits for them, and re-layouts: 1.26 us -> 0.58 us
    pallas_call x1, Pallas kernels: 39.1 us -> 38.6 us  [per_device(): pl.pallas_call(functools.partial(kernel, nodes, slabs, inner, nx * slabs...]
where the time goes in v5:
time: 39.5 us; the launch traced here: 39.1 us
  Pallas kernels  38.6 us (98%)
  local copies, waits for them, and re-layouts  0.58 us (1%)
    pallas_call x1, Pallas kernels, per_device(): pl.pallas_call(functools.partial(kernel, nodes, slabs, inner, nx * slabs...  38.6 us

profile of v5, /device:TPU:1, one launch (start us, length us, event | category | flops | bytes accessed | tf_op | source)
XLA Modules:
  0.0 39.1 jit_solution(4134136691286962371)
XLA Ops:
  0.0 38.6 %shard_map.55 = f32[4,32]{1,0:T(4,128)S(1)} custom-call(f32[1,6,4,64,256]{4,3,2,1,0:T(8,128)} %source.1, f32[1,4,4,64,256]{4,3,2,1,0:T(8,128)} %coef.1, f32[6,1,6]{2,1,0:T(1,128)} %bitcast.1, f32[1,6,4,64,256]{4,3,2,1,0:T(8,128)} %shape.1, f32[1,4,256]{2,1,0:T(4,128)} %wall.1), custom_call_target="tpu_custom_call" | custom-call | tf_op jit(solution)/shard_map/pallas_call | solution.py:412
  38.6 0.6 %copy.7 = f32[4,32]{1,0:T(4,128)} copy(f32[4,32]{1,0:T(4,128)S(1)} %shard_map.55) | data formatting | bytes 1024

commit v6 on v5

--- a/solution.py
+++ b/solution.py
@@ -36,7 +36,7 @@
     nodes, slabs, inner, cells,
     source, coef, flux_in, shape, wall, out,
     flux, psi0, cf, psi1, mix, tv, halo0, halo1, gsend, gheld, rsend, rheld, plain, aheld, acc, wallv, obj, own, sens, fin,
-    load_sem, turn_send, turn_recv, send0, recv0, send1, recv1, obj_send, obj_recv, fin_send, fin_recv,
+    entered, load_sem, turn_send, turn_recv, send0, recv0, send1, recv1, obj_send, obj_recv, fin_send, fin_recv,
 ):
     me, nd = lax.axis_index("slab"), lax.axis_index("node")
     outer = slabs // inner
@@ -59,7 +59,23 @@
 
     pl.when(has_left & (place == 0))(lambda: greet(left))
     pl.when(has_right & (place == inner - 1))(lambda: greet(right))
-    everyone = peers[0] + peers[1] + peers[2]
+    near = list(peers[2]) if nodes < 8 else [
+        {"node": nd + 1 - 2 * lax.rem(nd, 2)},
+        {"node": lax.rem(nd + 2, nodes)},
+        {"node": lax.rem(nd + nodes - 2, nodes)},
+    ]
+    if outer < 8:
+        near += peers[1]
+    else:
+        half = outer // 2
+        row, line = lax.div(group, half), lax.rem(group, half)
+        for spot in (
+            row * half + lax.rem(line + 1, half),
+            row * half + lax.rem(line + half - 1, half),
+            (1 - row) * half + line,
+        ):
+            near.append({"slab": spot * inner + place})
+    everyone = peers[0] + near
     for peer in everyone:
         greet(peer)
     beyond = jnp.where(has_left & (place == 0), 1, 0) + jnp.where(has_right & (place == inner - 1), 1, 0)
@@ -84,6 +100,13 @@
     load("flux", flux_in, flux)
     load("shape", shape.at[0], tv)
     order = [0, nx - 1] + list(range(1, nx - 1))
+
+    def tell(k):
+        for peer in near:
+            pl.semaphore_signal(entered.at[k], inc=1, device_id=peer, device_id_type=MESH)
+
+    def hear(k):
+        pl.semaphore_wait(entered.at[k], len(near))
 
     started = []
 
@@ -172,6 +195,9 @@
             plain_copy(c).start()
 
     def turn():
+        loads["flux"].wait()
+        loads["shape"].wait()
+
         def step(i, carry):
             rows = pl.ds(pl.multiple_of(i * ROWS, ROWS), ROWS)
             a = cf[1, 0, rows, :]
@@ -190,8 +216,6 @@
             loads["source", x, k].wait()
     for x in (0, nx - 1):
         start_psi(x, 0, ny)
-    loads["flux"].wait()
-    loads["shape"].wait()
     pl.when(opens_row)(turn)
 
     pl.semaphore_wait(barrier, len(everyone) + beyond)
@@ -202,6 +226,7 @@
         if c == 0:
             stage_a = spread(0, place)
     pl.when(ends_row)(coupling.start)
+    tell(0)
     loads["coef"].wait()
     loads["source"].wait()
     for x in range(1, nx - 1):
@@ -235,9 +260,15 @@
             return carry
         lax.fori_loop(0, ny // ROWS, combine, 0)
 
+    others = jnp.logical_not(opens_row)
+    pl.when(others)(loads["flux"].wait)
     for x in order:
         first_sweep(x)
     pl.when(ends_row)(send_plain)
+    hear(0)
+    tell(1)
+
+    pl.when(others)(loads["shape"].wait)
 
     for x in range(nx):
         def adjoint(i, total_sum):
@@ -255,6 +286,7 @@
         acc[x] = lax.fori_loop(0, ny // ROWS, adjoint, jnp.zeros((8, nz), jnp.float32))
 
     own[1] = collect(0, stage_a)
+    hear(1)
     stage_b = spread(1, group)
 
     def join(came, goes, x, c):
@@ -315,7 +347,7 @@
             return total + fold_rows(cf[1, x, rows, :] * product)
         acc[x] = lax.fori_loop(0, part // ROWS, step, acc[x])
 
-    def add_answer():
+    def add_own():
         coupling.wait_recv()
 
         def step(i, total):
@@ -328,9 +360,13 @@
                     mixed = mixed + flux[v, 0, o] * held[v]
                 product = product + tv[o, 0, rows, :] * mixed
             return total + fold_rows(aheld[rows, :] * cf[1, 0, rows, :] * product)
-        added = lax.fori_loop(0, ny // ROWS, step, acc[0])
+        acc[0] = lax.fori_loop(0, ny // ROWS, step, acc[0])
+
+    def add_answer():
         to_right.wait_recv()
-        acc[0] = added + rheld[...]
+        acc[0] = acc[0] + rheld[...]
+
+    pl.when(opens_row)(add_own)
 
     for c in range(CHUNKS):
         for came, goes, x, there in sides:
@@ -435,6 +471,7 @@
                 pltpu.VMEM((2, 1, LANES), f32),
                 pltpu.VMEM((nz // LANES, 8, LANES), f32),
                 pltpu.VMEM((nodes, 8, LANES), f32),
+                pltpu.SemaphoreType.REGULAR((2,)),
                 dma((13,)),
                 dma((3,)),
                 dma((3,)),

time: 39.5 us -> 39.3 us (level)
  no operation moved by 1% of the time
where the time goes in v6:
time: 39.3 us; the launch traced here: 39.2 us
  Pallas kernels  38.6 us (98%)
  local copies, waits for them, and re-layouts  0.58 us (1%)
    pallas_call x1, Pallas kernels, per_device(): pl.pallas_call(functools.partial(kernel, nodes, slabs, inner, nx * slabs...  38.6 us

profile of v6, /device:TPU:1, one launch (start us, length us, event | category | flops | bytes accessed | tf_op | source)
XLA Modules:
  0.0 39.2 jit_solution(3117667881550112525)
XLA Ops:
  0.0 38.6 %shard_map.55 = f32[4,32]{1,0:T(4,128)S(1)} custom-call(f32[1,6,4,64,256]{4,3,2,1,0:T(8,128)} %source.1, f32[1,4,4,64,256]{4,3,2,1,0:T(8,128)} %coef.1, f32[6,1,6]{2,1,0:T(1,128)} %bitcast.1, f32[1,6,4,64,256]{4,3,2,1,0:T(8,128)} %shape.1, f32[1,4,256]{2,1,0:T(4,128)} %wall.1), custom_call_target="tpu_custom_call" | custom-call | tf_op jit(solution)/shard_map/pallas_call | solution.py:448
  38.6 0.6 %copy.7 = f32[4,32]{1,0:T(4,128)} copy(f32[4,32]{1,0:T(4,128)S(1)} %shard_map.55) | data formatting | bytes 1024
